TPU v7x, 128 devices: a whole 4x4x4 slice. The times are simulated.
128 devices in a mesh: aa: 16 (over y, x), ba: 8 (over z, core).
Axes of the slice: x: 4, y: 4, z: 4, core: 2. Of those that a mesh axis runs over, the one named last changes fastest.
Arguments:
- queries: bfloat16 [8, 128, 8192], P('ba', None, 'aa'), may hold values from -10 to 10
- new_kv: bfloat16 [8, 128, 2, 512], P('ba', 'aa'), may hold values from -4 to 4
- pool: bfloat16 [8, 192, 32, 2, 512], P('ba', 'aa'), may hold values from -4 to 4
- page_table: int32 [8, 64], P('ba', 'aa'), may hold values from 0 to 11, as said below
- ctx_len: int32 [8, 16], P('ba', 'aa'), may hold values from 1 to 128, as said below
- move_page: int32 [8, 112], P('ba', 'aa'), may hold values from 0 to 11, as said below
- move_dest: int32 [8, 112], P('ba', 'aa'), may hold values from 0 to 7, as said below
- append_page: int32 [8, 16], P('ba', 'aa'), may hold values from 0 to 11
Outputs:
- attended: bfloat16 [8, 128, 8192], P('ba', None, 'aa')
- pool_out: bfloat16 [8, 192, 32, 2, 512], P('ba', 'aa')
Inputs may be any that keep to these rules, and one draw needn't show every extreme that they name: `page_table`: the entries of one device are distinct pages of its pool and differ from its leaving pages and its append page. `ctx_len`: for each instance some index of aa holds exactly 128 live rows. `move_page`: the 7 entries of one device are distinct pages of its pool. `move_dest`: A device never names its own instance and names any one instance at most 2 times; for each index of aa one instance is named exactly 2 times by the device of every other instance.
All inputs are finite; a program needn't handle non-finite values.
Results may differ from a plain program's by a relative error of at most 0.0017.
Values may be sent and summed in bfloat16 or wider, within the bound.
No kernel may reach another device: no remote copies, remote signals or barrier semaphores. Data moves between devices by JAX's collectives and lax.ppermute only.
A program may use at most 64 MiB of HBM per device.

v0:
```python
import math
import jax
import jax.numpy as jnp
from jax import lax
from jax.sharding import PartitionSpec as P

HEAD_DIM = 128
MOST = 2
NEG_LARGE = -1e30


def in_one_piece(arrays, axis, split_dim, concat_dim, along):
    widths = [math.prod(a.shape[along:]) for a in arrays]
    both = jnp.concatenate(
        [a.reshape(*a.shape[:along], w) for a, w in zip(arrays, widths)], axis=along
    )
    filled = lax.all_to_all(both, axis, split_axis=split_dim, concat_axis=concat_dim, tiled=True)
    blocks = jnp.split(filled, [sum(widths[:k]) for k in range(1, len(widths))], axis=along)
    return tuple(
        (b.reshape(*filled.shape[:along], *a.shape[along:]) for a, b in zip(arrays, blocks))
    )


def from_everyone(value, axis):
    length = lax.axis_size(axis)
    return lax.all_to_all(
        jnp.broadcast_to(value[None], (length, *value.shape)), axis, 0, 0, tiled=True
    )


def taken_together(value, axis):
    return from_everyone(value, axis).max(axis=0)


def split_up(value, dim, length):
    lengths = value.shape
    blocks = value.reshape(*lengths[:dim], length, lengths[dim] // length, *lengths[dim + 1 :])
    return jnp.moveaxis(blocks, dim, 0)


def sum_at_owner(value, axis, dim):
    length = lax.axis_size(axis)
    blocks = lax.all_to_all(split_up(value, dim, length), axis, 0, 0, tiled=True)
    return jnp.sum(blocks, axis=0)


def in_one_piece_2(arrays, axis, dim, along):
    widths = [math.prod(a.shape[along:]) for a in arrays]
    both = jnp.concatenate(
        [a.reshape(*a.shape[:along], w) for a, w in zip(arrays, widths)], axis=along
    )
    filled = sum_at_owner(both, axis, dim)
    blocks = jnp.split(filled, [sum(widths[:k]) for k in range(1, len(widths))], axis=along)
    return tuple(
        (b.reshape(*filled.shape[:along], *a.shape[along:]) for a, b in zip(arrays, blocks))
    )


def block_plan(total_rows):
    counted = max(1, total_rows // 512)
    length = -(-total_rows // counted)
    length = -(-length // 8) * 8
    return (counted, length)


def combine_parts(former, latter):
    former_max, former_sum, former_out = former
    latter_max, latter_sum, latter_out = latter
    joint_max = jnp.maximum(former_max, latter_max)
    former_scale = jnp.exp(former_max - joint_max)
    latter_scale = jnp.exp(latter_max - joint_max)
    joint_sum = former_sum * former_scale + latter_sum * latter_scale
    joint_out = former_out * former_scale[..., None] + latter_out * latter_scale[..., None]
    return (joint_max, joint_sum, joint_out)


def attend_rows(query_heads, key_rows, visible):
    total_rows = key_rows.shape[0]
    counted, length = block_plan(total_rows)
    query_count, kv_heads, group_size, head_dim = query_heads.shape
    blocked_keys = key_rows.reshape(counted, length, 2, kv_heads, head_dim)
    blocked_mask = visible.reshape(query_count, counted, length).transpose(1, 0, 2)
    scale = 1.0 / math.sqrt(head_dim)

    def block_step(state_now, inputs):
        run_max, run_sum, run_out = state_now
        block_keys, block_mask = inputs
        scores = (
            jnp.einsum(
                "qkgd,rkd->qkgr", query_heads, block_keys[:, 0], preferred_element_type=jnp.float32
            )
            * scale
        )
        allowed = block_mask[:, None, None, :]
        scores = jnp.where(allowed, scores, NEG_LARGE)
        new_max = jnp.maximum(run_max, jnp.max(scores, axis=-1))
        weights = jnp.where(allowed, jnp.exp(scores - new_max[..., None]), 0.0)
        shrink = jnp.exp(run_max - new_max)
        new_sum = run_sum * shrink + jnp.sum(weights, axis=-1)
        block_values = block_keys[:, 1].astype(jnp.float32)
        new_out = run_out * shrink[..., None] + jnp.einsum(
            "qkgr,rkd->qkgd", weights, block_values, precision=lax.Precision.HIGHEST
        )
        return ((new_max, new_sum, new_out), None)

    start_state = (
        jnp.full((query_count, kv_heads, group_size), NEG_LARGE, jnp.float32),
        jnp.zeros((query_count, kv_heads, group_size), jnp.float32),
        jnp.zeros((query_count, kv_heads, group_size, head_dim), jnp.float32),
    )
    finished, _ = lax.scan(block_step, start_state, (blocked_keys, blocked_mask))
    return finished


def local(queries, new_kv, pool, page_table, ctx_len, move_page, move_dest, append_page):
    instances = lax.axis_size("ba")
    position = lax.axis_index("aa")
    pool_pages = pool[0]
    page_rows = pool_pages.shape[1]
    kv_width = pool_pages.shape[-1]
    kv_heads = kv_width // HEAD_DIM
    gathered = lax.all_gather(queries[0], "aa", axis=1, tiled=True)
    query_count = gathered.shape[0]
    query_heads = gathered.reshape(query_count, kv_heads, -1, HEAD_DIM)
    moved_ids = move_page[0]
    targets = move_dest[0]
    move_count = moved_ids.shape[0]
    counter = jnp.arange(move_count, dtype=jnp.int32)
    earlier = (counter[None, :] < counter[:, None]) & (targets[None, :] == targets[:, None])
    slot_index = targets * MOST + jnp.sum(earlier, axis=1)
    select = (jnp.arange(instances * MOST, dtype=jnp.int32)[:, None] == slot_index[None, :]).astype(
        jnp.bfloat16
    )
    picked = jnp.take(pool_pages, moved_ids, axis=0).reshape(move_count, -1)
    outgoing = jnp.dot(select, picked, preferred_element_type=jnp.float32).astype(jnp.bfloat16)
    outgoing = outgoing.reshape(instances, MOST, page_rows, 2, kv_width)
    occupied = (
        jnp.sum(select.astype(jnp.float32), axis=1).astype(jnp.bfloat16).reshape(instances, MOST)
    )
    incoming, arrived = in_one_piece((outgoing, occupied), "ba", 0, 0, 2)
    moved_rows = incoming.reshape(-1, 2, kv_width)
    moved_live = jnp.broadcast_to(
        (arrived > 0.5)[:, :, None], (instances, MOST, page_rows)
    ).reshape(-1)
    resident = jnp.take(pool_pages, page_table[0], axis=0).reshape(-1, 2, kv_width)
    resident_live = jnp.arange(resident.shape[0], dtype=jnp.int32) < ctx_len[0, 0]
    fresh_rows = new_kv[0]
    fresh_count = fresh_rows.shape[0]
    fresh_place = position * fresh_count + jnp.arange(fresh_count, dtype=jnp.int32)
    fresh_visible = fresh_place[None, :] <= jnp.arange(query_count, dtype=jnp.int32)[:, None]
    resident_visible = jnp.broadcast_to(
        resident_live[None, :], (query_count, resident_live.shape[0])
    )
    moved_visible = jnp.broadcast_to(moved_live[None, :], (query_count, moved_live.shape[0]))
    local_part = attend_rows(
        query_heads,
        jnp.concatenate([resident, fresh_rows], axis=0),
        jnp.concatenate([resident_visible, fresh_visible], axis=1),
    )
    moved_part = attend_rows(query_heads, moved_rows, moved_visible)
    partials = combine_parts(local_part, moved_part)
    run_max, run_sum, run_out = partials
    top_max = taken_together(run_max, "aa")
    rescale = jnp.exp(run_max - top_max)
    numerator = (run_out * rescale[..., None]).reshape(query_count, -1, HEAD_DIM)
    denominator = (run_sum * rescale).reshape(query_count, -1)
    numerator, denominator = in_one_piece_2((numerator, denominator), "aa", 1, 2)
    result = numerator / denominator[..., None]
    attended = result.reshape(1, query_count, -1).astype(jnp.bfloat16)
    zero = jnp.zeros((), jnp.int32)
    updated = lax.dynamic_update_slice(
        pool_pages, fresh_rows[None], (append_page[0, 0], zero, zero, zero)
    )
    return (attended, updated[None])


def solution(mesh):
    return jax.shard_map(
        local,
        mesh=mesh,
        in_specs=(
            P("ba", None, "aa"),
            P("ba", "aa", None, None),
            P("ba", "aa", None, None, None),
            P("ba", "aa"),
            P("ba", "aa"),
            P("ba", "aa"),
            P("ba", "aa"),
            P("ba", "aa"),
        ),
        out_specs=(P("ba", None, "aa"), P("ba", "aa", None, None, None)),
        check_vma=False,
    )
```

profile of v0, /device:TPU:0, one launch (start us, length us, event | category | flops | bytes accessed | tf_op | source)
XLA Modules:
  0.0 190.3 jit_solution(174172654630481055)
XLA Ops:
  7.2 0.0 all-gather.3.cloned.1.call-start
  7.2 1.1 copy.173
  8.3 1.7 copy.132
  10.0 0.0 all-gather.3.cloned.1.call-update
  10.0 0.7 fusion.45
  10.7 0.7 compare_and_fusion
  11.4 0.9 convert_reduce_fusion
  12.3 0.7 fusion.46
  12.9 0.1 fusion.42
  13.0 0.1 reshape_reshape.9
  13.1 1.5 gather_fusion.1
  14.6 0.0 copy-start.4
  14.6 0.0 copy-start.3
  14.6 0.3 gather.15
  14.9 0.6 convolution_convert_fusion
  15.5 0.7 reshape_reshape.7
  16.2 1.9 %pad_maximum_fusion = bf16[8,2,32769]{2,1,0:T(2,128)(2,1)} fusion(bf16[8,2,1]{2,1,0:T(2,128)(2,1)S(1)} %reshape_reshape.9, bf16[8,2,32768]{2,1,0:T(2,128)(2,1)S(1)} %reshape_reshape.7), kind=kLoop, calls=%fused_computation.33 | loop fusion | flops 2097216 | bytes 2097216 | tf_op jit(solution)/shard_map/concatenate | solution.py:14
  18.2 5.4 %all-to-all-start = ((bf16[8,2,32769]{2,1,0:T(2,128)(2,1)}), bf16[8,2,32769]{2,1,0:T(2,128)(2,1)S(1)}, u32[]{:S(2)}, u32[]{:S(2)}) async-start(bf16[8,2,32769]{2,1,0:T(2,128)(2,1)} %pad_maximum_fusion), calls=%async_computation | async-start | bytes 2105344 | tf_op jit(solution)/shard_map/all_to_all | solution.py:17
  23.6 0.0 copy-done.4
  24.3 0.1 broadcast_in_dim.123
  24.4 0.1 broadcast_in_dim.124
  24.4 0.0 copy-done.3
  24.5 1.1 gather_fusion
  25.6 0.2 reshape.297
  25.8 0.1 iota_compare_fusion.3
  25.8 0.1 pad_add_fusion
  25.9 0.1 copy_select_fusion
  26.0 13.6 %all-to-all-done = bf16[8,2,32769]{2,1,0:T(2,128)(2,1)S(1)} async-done(((bf16[8,2,32769]{2,1,0:T(2,128)(2,1)}), bf16[8,2,32769]{2,1,0:T(2,128)(2,1)S(1)}, u32[]{:S(2)}, u32[]{:S(2)}) %all-to-all-start) | async-done | bytes 1048640 | tf_op jit(solution)/shard_map/all_to_all | solution.py:17
  39.6 0.1 copy.156
  39.7 0.7 split.17
  40.4 0.8 squeeze.63
  41.3 0.4 fusion.58
  41.6 1.1 copy.158
  42.8 0.1 copy.136
  42.9 0.1 broadcast_in_dim.132
  42.9 0.1 broadcast_in_dim.133
  43.0 15.0 %all-gather.3.cloned.1.call-done = bf16[1,128,8192]{1,2,0:T(8,128)(2,1)} async-done(((bf16[1,128,512]{1,2,0:T(8,128)(2,1)}), bf16[1,128,8192]{1,2,0:T(8,128)(2,1)}) %all-gather.3.cloned.1.call-update) | async-done | bytes 2097168 | tf_op jit(solution)/shard_map/all_gather | solution.py:122
  58.0 0.0 copy-start
  58.1 8.9 %bitcast_reduce_fusion = (f32[128,4,16]{0,2,1:T(8,128)S(1)}, f32[4,512,128,16]{2,1,3,0:T(8,128)}) fusion(pred[512]{0:T(512)(128)(4,1)S(1)} %broadcast_in_dim.133, bf16[128,4,16,128]{0,3,2,1:T(8,128)(2,1)} %bitcast.111, bf16[512,1,4,128]{3,2,1,0:T(4,128)(2,1)S(1)} %get-tuple-element.59), kind=kOutput, calls=%fused_computation.4 | convolution fusion | flops 1086316544 | bytes 19431936 | tf_op jit(solution)/shard_map/while/body/eval_jaxpr/qkgd,rkd->qkgr/dot_general | solution.py:89
  66.9 0.0 copy-done
  66.9 2.9 %fusion.15 = (f32[128,4,16]{0,2,1:T(8,128)S(1)}, f32[4,136,128,16]{2,1,3,0:T(8,128)}) fusion(pred[128,136]{0,1:T(8,128)(4,1)S(1)} %pad_add_fusion, bf16[128,4,16,128]{0,3,2,1:T(8,128)(2,1)S(1)} %bitcast.112, bf16[128,2,4,128]{3,0,2,1:T(8,128)(2,1)S(1)} %copy_select_fusion, bf16[8,2,4,128]{3,0,2,1:T(8,128)(2,1)S(1)} %copy.131), kind=kOutput, calls=%fused_computation.25 | convolution fusion | flops 288825344 | bytes 6882304 | tf_op jit(solution)/shard_map/while/body/eval_jaxpr/qkgd,rkd->qkgr/dot_general | solution.py:89
  69.8 0.8 broadcast_in_dim.138
  70.7 0.0 slice-start
  70.7 5.1 %all-to-all-start.1 = ((f32[16,128,4,16]{1,3,2,0:T(8,128)}), f32[16,128,4,16]{1,3,2,0:T(8,128)S(1)}, u32[]{:S(2)}, u32[]{:S(2)}) async-start(f32[16,128,4,16]{1,3,2,0:T(8,128)} %broadcast_in_dim.138), calls=%async_computation.1 | async-start | bytes 1048576 | tf_op jit(solution)/shard_map/all_to_all | solution.py:26
  75.8 0.0 slice-start.1
  75.8 8.5 %fusion.2 = f32[128,4,16]{0,2,1:T(8,128)S(1)} fusion(f32[4,512,128,16]{2,1,3,0:T(8,128)} %get-tuple-element.69, f32[128,4,16]{0,2,1:T(8,128)S(1)} %get-tuple-element.62, pred[512]{0:T(512)(128)(4,1)S(1)} %broadcast_in_dim.133), kind=kLoop, calls=%fused_computation.8 | loop fusion | flops 20963328 | bytes 16843264 | tf_op jit(solution)/shard_map/while/body/eval_jaxpr/reduce_sum | solution.py:99
  84.3 0.0 slice-done
  84.3 0.0 slice-done.1
  84.3 1.3 fusion.16
  85.6 0.0 copy-start.2
  85.7 5.3 %fusion.17 = f32[4,128,128,16]{2,1,3,0:T(8,128)} fusion(f32[4,136,128,16]{2,1,3,0:T(8,128)S(1)} %bitcast.110, f32[128,4,16]{0,2,1:T(8,128)S(1)} %get-tuple-element.65, pred[128,136]{0,1:T(8,128)(4,1)S(1)} %pad_add_fusion, bf16[8,2,4,128]{3,0,2,1:T(8,128)(2,1)S(1)} %copy.131, bf16[128,2,4,128]{3,0,2,1:T(8,128)(2,1)S(1)} %copy_select_fusion), kind=kOutput, calls=%fused_computation.27 | convolution fusion | flops 1716011008 | bytes 8979456 | tf_op jit(solution)/shard_map/while/body/eval_jaxpr/qkgr,rkd->qkgd/dot_general | solution.py:101
  90.9 0.0 all-to-all-done.1
  91.0 0.0 copy-done.2
  91.0 15.8 %fusion.13 = f32[128,4,16,128]{0,3,2,1:T(8,128)S(1)} fusion(f32[4,128,128,16]{2,1,3,0:T(8,128)} %fusion.17, f32[4,512,128,16]{2,1,3,0:T(8,128)} %get-tuple-element.69, f32[128,4,16]{0,2,1:T(8,128)S(1)} %get-tuple-element.62, pred[512]{0:T(512)(128)(4,1)S(1)} %broadcast_in_dim.133, f32[128,4,16]{0,2,1:T(8,128)S(1)} %get-tuple-element.64, ...), kind=kOutput, calls=%fused_computation.22 | convolution fusion | flops 6465519616 | bytes 25887232 | tf_op jit(solution)/shard_map/while/body/eval_jaxpr/qkgr,rkd->qkgd/dot_general | solution.py:101
  106.8 2.8 %copy.141 = f32[128,16,4,128]{0,2,3,1:T(4,128)S(1)} copy(f32[128,16,4,128]{0,3,2,1:T(8,128)S(1)} %bitcast.113) | data formatting | bytes 8388608 | tf_op jit(solution)/shard_map/concatenate | solution.py:49
  109.6 0.1 exponential_multiply_fusion
  109.6 3.0 %maximum_bitcast_fusion = f32[16,128,4,129]{1,2,3,0:T(4,128)} fusion(f32[128,16,4,1]{0,2,3,1:T(4,128)S(1)} %exponential_multiply_fusion, f32[128,16,4,128]{0,2,3,1:T(4,128)S(1)} %copy.141), kind=kLoop, calls=%fused_computation.18 | loop fusion | flops 1056768 | bytes 8454144 | tf_op jit(solution)/shard_map/transpose | solution.py:38
  112.6 7.3 %all-to-all-start.2 = ((f32[16,128,4,129]{1,2,3,0:T(4,128)}), f32[16,128,4,129]{1,2,3,0:T(4,128)}, u32[]{:S(2)}, u32[]{:S(2)}) async-start(f32[16,128,4,129]{1,2,3,0:T(4,128)} %maximum_bitcast_fusion), calls=%async_computation.2 | async-start | bytes 8454144 | tf_op jit(solution)/shard_map/all_to_all | solution.py:43
  120.5 0.0 copy-start.1
  120.5 59.2 %all-to-all-done.2 = f32[16,128,4,129]{1,2,3,0:T(4,128)} async-done(((f32[16,128,4,129]{1,2,3,0:T(4,128)}), f32[16,128,4,129]{1,2,3,0:T(4,128)}, u32[]{:S(2)}, u32[]{:S(2)}) %all-to-all-start.2) | async-done | bytes 4227104 | tf_op jit(solution)/shard_map/all_to_all | solution.py:43
  179.7 2.9 %reduce_sum.63 = f32[128,4,129]{0,1,2:T(4,128)S(1)} reduce(f32[16,128,4,129]{1,2,3,0:T(4,128)} %all-to-all-done.2, f32[]{:T(128)} %constant.52.clone.1), dimensions={0}, to_apply=%region_7.8 | reduce | flops 990720 | bytes 4491268 | tf_op jit(solution)/shard_map/reduce_sum | solution.py:44
  182.6 0.8 copy.143
  183.4 0.0 copy-done.1
  (19 shorter events, 0.2 us)
Async XLA Ops:
  7.2 50.9 %all-gather.3.cloned.1.call-start = ((), (), s32[]{:S(2)}) async-start(), calls=%async_computation.3 | async-start | bytes 2228224 | tf_op jit(solution)/shard_map/all_gather | solution.py:122
  14.6 9.0 %copy-start.4 = (s32[1,4]{1,0:T(1,128)S(1)}, s32[1,4]{1,0:T(1,128)}, u32[]{:S(2)}) copy-start(s32[1,4]{1,0:T(1,128)} %param.11) | copy-start | bytes 52
  14.6 9.8 %copy-start.3 = (bf16[1,8,2,512]{3,2,1,0:T(2,128)(2,1)S(1)}, bf16[1,8,2,512]{3,2,1,0:T(2,128)(2,1)}, u32[]{:S(2)}) copy-start(bf16[1,8,2,512]{3,2,1,0:T(2,128)(2,1)} %param.9) | copy-start | bytes 49156
  18.2 21.4 %all-to-all-start = ((bf16[8,2,32769]{2,1,0:T(2,128)(2,1)}), bf16[8,2,32769]{2,1,0:T(2,128)(2,1)S(1)}, u32[]{:S(2)}, u32[]{:S(2)}) async-start(bf16[8,2,32769]{2,1,0:T(2,128)(2,1)} %pad_maximum_fusion), calls=%async_computation | async-start | bytes 2105344 | tf_op jit(solution)/shard_map/all_to_all | solution.py:17
  58.0 8.9 %copy-start = (bf16[1,128,8192]{1,2,0:T(8,128)(2,1)S(1)}, bf16[1,128,8192]{1,2,0:T(8,128)(2,1)}, u32[]{:S(2)}) copy-start(bf16[1,128,8192]{1,2,0:T(8,128)(2,1)} %all-gather.3.cloned.1.call-done) | copy-start | bytes 6291460
  70.7 13.6 %slice-start = ((s8[4456448]{0:T(1024)(128)(4,1)}), s8[262144]{0:T(1024)(128)(4,1)S(1)}, s32[]{:S(2)}) async-start(s8[4456448]{0:T(1024)(128)(4,1)} %bitcast.109), calls=%async_computation.4 | async-start | bytes 524288
  70.7 20.2 %all-to-all-start.1 = ((f32[16,128,4,16]{1,3,2,0:T(8,128)}), f32[16,128,4,16]{1,3,2,0:T(8,128)S(1)}, u32[]{:S(2)}, u32[]{:S(2)}) async-start(f32[16,128,4,16]{1,3,2,0:T(8,128)} %broadcast_in_dim.138), calls=%async_computation.1 | async-start | bytes 1048576 | tf_op jit(solution)/shard_map/all_to_all | solution.py:26
  75.8 8.6 %slice-start.1 = ((s8[4456448]{0:T(1024)(128)(4,1)}), s8[4194304]{0:T(1024)(128)(4,1)S(1)}, s32[]{:S(2)}) async-start(s8[4456448]{0:T(1024)(128)(4,1)} %bitcast.109), calls=%async_computation.5 | async-start | bytes 8388608
  85.6 5.3 %copy-start.2 = (bf16[512,1,4,128]{0,3,2,1:T(8,128)(2,1)S(1)}, bf16[512,1,4,128]{0,3,2,1:T(8,128)(2,1)}, u32[]{:S(2)}) copy-start(bf16[512,1,4,128]{0,3,2,1:T(8,128)(2,1)} %copy.158) | copy-start | bytes 1572868
  112.6 67.1 %all-to-all-start.2 = ((f32[16,128,4,129]{1,2,3,0:T(4,128)}), f32[16,128,4,129]{1,2,3,0:T(4,128)}, u32[]{:S(2)}, u32[]{:S(2)}) async-start(f32[16,128,4,129]{1,2,3,0:T(4,128)} %maximum_bitcast_fusion), calls=%async_computation.2 | async-start | bytes 8454144 | tf_op jit(solution)/shard_map/all_to_all | solution.py:43
  120.5 62.9 %copy-start.1 = (bf16[1,12,32,2,512]{4,3,2,1,0:T(2,128)(2,1)}, bf16[1,12,32,2,512]{4,3,2,1,0:T(2,128)(2,1)S(1)}, u32[]{:S(2)}) copy-start(bf16[1,12,32,2,512]{4,3,2,1,0:T(2,128)(2,1)S(1)} %bitcast_dynamic-update-slice_fusion) | copy-start | bytes 2359300
Sparse Core Ops, SparseCore 0:
  10.7 47.2 all-gather.2
where the time goes:
time: 191 us; the launch traced here: 190 us
  waiting for transfers between devices  87.8 us (46%)
  matrix products  33.4 us (17%)
  other arithmetic  21 us (11%)
  starting transfers between devices  17.8 us (9%)
  between operations  15.6 us (8%)
  local copies, waits for them, and re-layouts  14.7 us (8%)
    all_to_all x1, waiting for transfers between devices, sum_at_owner(): lax.all_to_all(split_up(value, dim, length), axis, 0, 0, tiled=True)  59.2 us
    dot_general x2, matrix products, block_step(): jnp.einsum('qkgr,rkd->qkgd', weights, block_values, precision=lax.Precisi...  21 us
    all_gather x1, waiting for transfers between devices, local(): gathered = lax.all_gather(queries[0], 'aa', axis=1, tiled=True)  15 us
    all_to_all x1, waiting for transfers between devices, in_one_piece(): lax.all_to_all(both, axis, split_axis=split_dim, concat_axis=concat_dim,...  13.6 us
    dot_general x2, matrix products, block_step(): jnp.einsum('qkgd,rkd->qkgr', query_heads, block_keys[:, 0], preferred_ele...  11.8 us
    reduce_sum x2, other arithmetic, block_step(): new_sum = run_sum * shrink + jnp.sum(weights, axis=-1)  9.83 us
    all_to_all x1, starting transfers between devices, sum_at_owner(): lax.all_to_all(split_up(value, dim, length), axis, 0, 0, tiled=True)  7.25 us
    all_to_all x1, starting transfers between devices, in_one_piece(): lax.all_to_all(both, axis, split_axis=split_dim, concat_axis=concat_dim,...  5.39 us
  transfers between devices with their start and end apart: 4, of which 3 were waited for; matrix products, arithmetic and copies ran while one was open for 15% of the time, Pallas kernels for 0%

commit v1 on v0

--- a/solution.py
+++ b/solution.py
@@ -119,7 +119,12 @@
     page_rows = pool_pages.shape[1]
     kv_width = pool_pages.shape[-1]
     kv_heads = kv_width // HEAD_DIM
-    gathered = lax.all_gather(queries[0], "aa", axis=1, tiled=True)
+    ring = [queries[0]]
+    for hop in range(15):
+        ring.append(lax.ppermute(ring[-1], "aa", [(dev, (dev + 1) % 16) for dev in range(16)]))
+    gathered = jnp.roll(
+        jnp.concatenate(ring[::-1], axis=1), (lax.axis_index("aa") + 1) * ring[0].shape[1], axis=1
+    )
     query_count = gathered.shape[0]
     query_heads = gathered.reshape(query_count, kv_heads, -1, HEAD_DIM)
     moved_ids = move_page[0]

time: 191 us -> 260 us (1.36)
  waiting for transfers between devices: 87.8 us -> 153 us
  local copies, waits for them, and re-layouts: 14.7 us -> 30.6 us
  between operations: 15.6 us -> 2.64 us
    ppermute x0 -> x15, waiting for transfers between devices: none -> 106 us  [local(): lax.ppermute(ring[-1], 'aa', [(dev, (dev + 1) % 16) for dev in range(16)])]
    all_gather x1 -> x0, waiting for transfers between devices: 15 us -> none  [local(): gathered = lax.all_gather(queries[0], 'aa', axis=1, tiled=True)]
    unnamed x19 -> x86, local copies, waits for them, and re-layouts: 4.82 us -> 18.6 us
    all_to_all x1, waiting for transfers between devices: 13.6 us -> 0.01 us  [in_one_piece(): lax.all_to_all(both, axis, split_axis=split_dim, concat_axis=concat_dim,...]
    all_to_all x1, waiting for transfers between devices: 59.2 us -> 47.2 us  [sum_at_owner(): lax.all_to_all(split_up(value, dim, length), axis, 0, 0, tiled=True)]
  transfers between devices with their start and end apart: 4 -> 18, of which waited for: 3 -> 16; matrix products, arithmetic and copies ran while one was open for 15% -> 12% of each run, Pallas kernels for 0% -> 0%
where the time goes in v1:
time: 260 us; the launch traced here: 259 us
  waiting for transfers between devices  153 us (59%)
  matrix products  31.9 us (12%)
  local copies, waits for them, and re-layouts  30.6 us (12%)
  other arithmetic  22.4 us (9%)
  starting transfers between devices  18 us (7%)
  between operations  2.64 us (1%)
    ppermute x15, waiting for transfers between devices, local(): lax.ppermute(ring[-1], 'aa', [(dev, (dev + 1) % 16) for dev in range(16)])  106 us
    all_to_all x1, waiting for transfers between devices, sum_at_owner(): lax.all_to_all(split_up(value, dim, length), axis, 0, 0, tiled=True)  47.2 us
    dot_general x2, matrix products, block_step(): jnp.einsum('qkgr,rkd->qkgd', weights, block_values, precision=lax.Precisi...  21.1 us
    unnamed x86, local copies, waits for them, and re-layouts  18.6 us
    dot_general x2, matrix products, block_step(): jnp.einsum('qkgd,rkd->qkgr', query_heads, block_keys[:, 0], preferred_ele...  10.2 us
    reduce_sum x2, other arithmetic, block_step(): new_sum = run_sum * shrink + jnp.sum(weights, axis=-1)  9.9 us
    all_to_all x1, starting transfers between devices, sum_at_owner(): lax.all_to_all(split_up(value, dim, length), axis, 0, 0, tiled=True)  7.12 us
    all_to_all x1, starting transfers between devices, in_one_piece(): lax.all_to_all(both, axis, split_axis=split_dim, concat_axis=concat_dim,...  5.32 us
  transfers between devices with their start and end apart: 18, of which 16 were waited for; matrix products, arithmetic and copies ran while one was open for 12% of the time, Pallas kernels for 0%

profile of v1, /device:TPU:0, one launch (start us, length us, event | category | flops | bytes accessed | tf_op | source)
XLA Modules:
  0.0 258.8 jit_solution(14975823950791445954)
XLA Ops:
  0.6 1.1 copy.204
  1.8 1.1 copy.132
  2.9 1.6 collective-permute-start
  4.6 7.2 %collective-permute-done = bf16[128,512]{0,1:T(8,128)(2,1)S(1)} collective-permute-done((bf16[128,512]{0,1:T(8,128)(2,1)S(1)}, bf16[128,512]{0,1:T(8,128)(2,1)S(1)}, u32[]{:S(2)}, u32[]{:S(2)}) %collective-permute-start) | collective-permute-done | bytes 131104 | tf_op jit(solution)/shard_map/ppermute | solution.py:124
  11.8 0.7 fusion.44
  12.4 7.6 %collective-permute-done.1 = bf16[128,512]{0,1:T(8,128)(2,1)S(1)} collective-permute-done((bf16[128,512]{0,1:T(8,128)(2,1)S(1)}, bf16[128,512]{0,1:T(8,128)(2,1)S(1)}, u32[]{:S(2)}, u32[]{:S(2)}) %collective-permute-start.1) | collective-permute-done | bytes 131104 | tf_op jit(solution)/shard_map/ppermute | solution.py:124
  20.1 0.7 fusion.45
  20.7 7.6 %collective-permute-done.2 = bf16[128,512]{0,1:T(8,128)(2,1)S(1)} collective-permute-done((bf16[128,512]{0,1:T(8,128)(2,1)S(1)}, bf16[128,512]{0,1:T(8,128)(2,1)S(1)}, u32[]{:S(2)}, u32[]{:S(2)}) %collective-permute-start.2) | collective-permute-done | bytes 131104 | tf_op jit(solution)/shard_map/ppermute | solution.py:124
  28.4 1.5 gather_fusion.1
  30.2 0.9 convert_reduce_fusion
  31.1 5.6 %collective-permute-done.3 = bf16[128,512]{0,1:T(8,128)(2,1)S(1)} collective-permute-done((bf16[128,512]{0,1:T(8,128)(2,1)S(1)}, bf16[128,512]{0,1:T(8,128)(2,1)S(1)}, u32[]{:S(2)}, u32[]{:S(2)}) %collective-permute-start.3) | collective-permute-done | bytes 131104 | tf_op jit(solution)/shard_map/ppermute | solution.py:124
  36.6 0.7 fusion.46
  37.3 7.6 %collective-permute-done.4 = bf16[128,512]{0,1:T(8,128)(2,1)S(1)} collective-permute-done((bf16[128,512]{0,1:T(8,128)(2,1)S(1)}, bf16[128,512]{0,1:T(8,128)(2,1)S(1)}, u32[]{:S(2)}, u32[]{:S(2)}) %collective-permute-start.4) | collective-permute-done | bytes 131104 | tf_op jit(solution)/shard_map/ppermute | solution.py:124
  44.9 0.7 compare_and_fusion
  45.6 8.0 %collective-permute-done.5 = bf16[128,512]{0,1:T(8,128)(2,1)} collective-permute-done((bf16[128,512]{0,1:T(8,128)(2,1)S(1)}, bf16[128,512]{0,1:T(8,128)(2,1)}, u32[]{:S(2)}, u32[]{:S(2)}) %collective-permute-start.5) | collective-permute-done | bytes 131104 | tf_op jit(solution)/shard_map/ppermute | solution.py:124
  54.4 0.7 reshape_reshape.7
  55.1 8.5 %collective-permute-done.6 = bf16[128,512]{0,1:T(8,128)(2,1)} collective-permute-done((bf16[128,512]{0,1:T(8,128)(2,1)}, bf16[128,512]{0,1:T(8,128)(2,1)}, u32[]{:S(2)}, u32[]{:S(2)}) %collective-permute-start.6) | collective-permute-done | bytes 131104 | tf_op jit(solution)/shard_map/ppermute | solution.py:124
  63.6 1.9 pad_maximum_fusion
  65.5 5.3 %all-to-all-start = ((bf16[8,2,32769]{2,1,0:T(2,128)(2,1)}), bf16[8,2,32769]{2,1,0:T(2,128)(2,1)S(1)}, u32[]{:S(2)}, u32[]{:S(2)}) async-start(bf16[8,2,32769]{2,1,0:T(2,128)(2,1)} %pad_maximum_fusion), calls=%async_computation | async-start | bytes 2105344 | tf_op jit(solution)/shard_map/all_to_all | solution.py:17
  70.9 1.2 collective-permute-done.7
  73.0 1.1 gather_fusion
  74.2 6.2 %collective-permute-done.8 = bf16[128,512]{0,1:T(8,128)(2,1)S(1)} collective-permute-done((bf16[128,512]{0,1:T(8,128)(2,1)S(1)}, bf16[128,512]{0,1:T(8,128)(2,1)S(1)}, u32[]{:S(2)}, u32[]{:S(2)}) %collective-permute-start.8) | collective-permute-done | bytes 131104 | tf_op jit(solution)/shard_map/ppermute | solution.py:124
  80.6 8.2 %collective-permute-done.9 = bf16[128,512]{0,1:T(8,128)(2,1)S(1)} collective-permute-done((bf16[128,512]{0,1:T(8,128)(2,1)S(1)}, bf16[128,512]{0,1:T(8,128)(2,1)S(1)}, u32[]{:S(2)}, u32[]{:S(2)}) %collective-permute-start.9) | collective-permute-done | bytes 131104 | tf_op jit(solution)/shard_map/ppermute | solution.py:124
  88.8 0.8 reshape.296
  89.5 0.6 copy.131
  90.2 6.9 %collective-permute-done.10 = bf16[128,512]{0,1:T(8,128)(2,1)S(1)} collective-permute-done((bf16[128,512]{0,1:T(8,128)(2,1)S(1)}, bf16[128,512]{0,1:T(8,128)(2,1)S(1)}, u32[]{:S(2)}, u32[]{:S(2)}) %collective-permute-start.10) | collective-permute-done | bytes 131104 | tf_op jit(solution)/shard_map/ppermute | solution.py:124
  97.1 8.3 %collective-permute-done.11 = bf16[128,512]{0,1:T(8,128)(2,1)} collective-permute-done((bf16[128,512]{0,1:T(8,128)(2,1)S(1)}, bf16[128,512]{0,1:T(8,128)(2,1)}, u32[]{:S(2)}, u32[]{:S(2)}) %collective-permute-start.11) | collective-permute-done | bytes 131104 | tf_op jit(solution)/shard_map/ppermute | solution.py:124
  105.4 0.7 pad_add_fusion
  106.2 0.7 split.17
  106.9 0.8 squeeze.63
  107.7 6.3 %collective-permute-done.12 = bf16[128,512]{0,1:T(8,128)(2,1)} collective-permute-done((bf16[128,512]{0,1:T(8,128)(2,1)}, bf16[128,512]{0,1:T(8,128)(2,1)}, u32[]{:S(2)}, u32[]{:S(2)}) %collective-permute-start.12) | collective-permute-done | bytes 131104 | tf_op jit(solution)/shard_map/ppermute | solution.py:124
  114.9 8.5 %collective-permute-done.13 = bf16[128,512]{0,1:T(8,128)(2,1)} collective-permute-done((bf16[128,512]{0,1:T(8,128)(2,1)}, bf16[128,512]{0,1:T(8,128)(2,1)}, u32[]{:S(2)}, u32[]{:S(2)}) %collective-permute-start.13) | collective-permute-done | bytes 131104 | tf_op jit(solution)/shard_map/ppermute | solution.py:124
  123.8 8.2 %collective-permute-done.14 = bf16[128,512]{0,1:T(8,128)(2,1)S(1)} collective-permute-done((bf16[128,512]{0,1:T(8,128)(2,1)}, bf16[128,512]{0,1:T(8,128)(2,1)S(1)}, u32[]{:S(2)}, u32[]{:S(2)}) %collective-permute-start.14) | collective-permute-done | bytes 131104 | tf_op jit(solution)/shard_map/ppermute | solution.py:124
  132.0 0.9 constant_dynamic-update-slice_fusion.30
  132.9 0.9 constant_dynamic-update-slice_fusion.29
  133.8 0.9 constant_dynamic-update-slice_fusion.28
  134.8 0.9 constant_dynamic-update-slice_fusion.27
  135.7 0.9 constant_dynamic-update-slice_fusion.26
  136.6 0.9 constant_dynamic-update-slice_fusion.25
  137.5 0.9 constant_dynamic-update-slice_fusion.24
  138.5 0.9 constant_dynamic-update-slice_fusion.23
  139.4 0.9 constant_dynamic-update-slice_fusion.22
  140.3 0.9 constant_dynamic-update-slice_fusion.21
  141.3 0.9 constant_dynamic-update-slice_fusion.20
  142.3 0.9 constant_dynamic-update-slice_fusion.14
  143.3 0.9 constant_dynamic-update-slice_fusion.13
  144.2 0.9 constant_dynamic-update-slice_fusion.12
  145.3 0.9 constant_dynamic-update-slice_fusion.7
  146.2 0.9 constant_dynamic-update-slice_fusion.6
  147.5 7.3 %bitcast_reduce_fusion = (f32[128,4,16]{0,2,1:T(8,128)S(1)}, f32[4,512,128,16]{2,1,3,0:T(8,128)}) fusion(pred[512]{0:T(512)(128)(4,1)S(1)} %broadcast_in_dim.133, bf16[128,4,16,128]{0,3,2,1:T(8,128)(2,1)S(1)} %bitcast.114, bf16[512,1,4,128]{3,2,1,0:T(4,128)(2,1)S(1)} %get-tuple-element.59), kind=kOutput, calls=%fused_computation.4 | convolution fusion | flops 1086316544 | bytes 19431936 | tf_op jit(solution)/shard_map/while/body/eval_jaxpr/qkgd,rkd->qkgr/dot_general | solution.py:89
  154.8 2.9 %fusion.15 = (f32[128,4,16]{0,2,1:T(8,128)S(1)}, f32[4,136,128,16]{2,1,3,0:T(8,128)}) fusion(pred[128,136]{0,1:T(8,128)(4,1)S(1)} %copy-done.19, bf16[128,4,16,128]{0,3,2,1:T(8,128)(2,1)S(1)} %bitcast.115, bf16[128,2,4,128]{3,0,2,1:T(8,128)(2,1)S(1)} %copy_select_fusion, bf16[8,2,4,128]{3,0,2,1:T(8,128)(2,1)S(1)} %copy-done.20), kind=kOutput, calls=%fused_computation.25 | convolution fusion | flops 288825344 | bytes 6882304 | tf_op jit(solution)/shard_map/while/body/eval_jaxpr/qkgd,rkd->qkgr/dot_general | solution.py:89
  157.7 0.9 broadcast_in_dim.138
  158.5 3.9 %all-to-all-start.1 = ((f32[16,128,4,16]{1,3,2,0:T(8,128)}), f32[16,128,4,16]{1,3,2,0:T(8,128)S(1)}, u32[]{:S(2)}, u32[]{:S(2)}) async-start(f32[16,128,4,16]{1,3,2,0:T(8,128)} %broadcast_in_dim.138), calls=%async_computation.1 | async-start | bytes 1048576 | tf_op jit(solution)/shard_map/all_to_all | solution.py:26
  162.5 8.6 %fusion.2 = f32[128,4,16]{0,2,1:T(8,128)S(1)} fusion(f32[4,512,128,16]{2,1,3,0:T(8,128)} %get-tuple-element.69, f32[128,4,16]{0,2,1:T(8,128)S(1)} %get-tuple-element.62, pred[512]{0:T(512)(128)(4,1)S(1)} %broadcast_in_dim.133), kind=kLoop, calls=%fused_computation.8 | loop fusion | flops 20963328 | bytes 16843264 | tf_op jit(solution)/shard_map/while/body/eval_jaxpr/reduce_sum | solution.py:99
  171.1 1.3 fusion.16
  172.4 5.3 %fusion.17 = f32[4,128,128,16]{2,1,3,0:T(8,128)} fusion(f32[4,136,128,16]{2,1,3,0:T(8,128)S(1)} %bitcast.113, f32[128,4,16]{0,2,1:T(8,128)S(1)} %get-tuple-element.65, pred[128,136]{0,1:T(8,128)(4,1)S(1)} %copy-done.19, bf16[8,2,4,128]{3,0,2,1:T(8,128)(2,1)S(1)} %copy-done.20, bf16[128,2,4,128]{3,0,2,1:T(8,128)(2,1)S(1)} %copy_select_fusion), kind=kOutput, calls=%fused_computation.27 | convolution fusion | flops 1716011008 | bytes 8979456 | tf_op jit(solution)/shard_map/while/body/eval_jaxpr/qkgr,rkd->qkgd/dot_general | solution.py:101
  177.8 15.8 %fusion.13 = f32[128,4,16,128]{0,3,2,1:T(8,128)S(1)} fusion(f32[4,128,128,16]{2,1,3,0:T(8,128)} %fusion.17, f32[4,512,128,16]{2,1,3,0:T(8,128)} %get-tuple-element.69, f32[128,4,16]{0,2,1:T(8,128)S(1)} %get-tuple-element.62, pred[512]{0:T(512)(128)(4,1)S(1)} %broadcast_in_dim.133, f32[128,4,16]{0,2,1:T(8,128)S(1)} %get-tuple-element.64, ...), kind=kOutput, calls=%fused_computation.22 | convolution fusion | flops 6465519616 | bytes 25887232 | tf_op jit(solution)/shard_map/while/body/eval_jaxpr/qkgr,rkd->qkgd/dot_general | solution.py:101
  193.6 2.8 %copy.141 = f32[128,16,4,128]{0,2,3,1:T(4,128)S(1)} copy(f32[128,16,4,128]{0,3,2,1:T(8,128)S(1)} %bitcast.116) | data formatting | bytes 8388608 | tf_op jit(solution)/shard_map/concatenate | solution.py:49
  196.5 3.0 %maximum_bitcast_fusion = f32[16,128,4,129]{1,2,3,0:T(4,128)} fusion(f32[128,16,4,1]{0,2,3,1:T(4,128)S(1)} %exponential_multiply_fusion, f32[128,16,4,128]{0,2,3,1:T(4,128)S(1)} %copy.141), kind=kLoop, calls=%fused_computation.18 | loop fusion | flops 1056768 | bytes 8454144 | tf_op jit(solution)/shard_map/transpose | solution.py:38
  199.5 7.1 %all-to-all-start.2 = ((f32[16,128,4,129]{1,2,3,0:T(4,128)}), f32[16,128,4,129]{1,2,3,0:T(4,128)}, u32[]{:S(2)}, u32[]{:S(2)}) async-start(f32[16,128,4,129]{1,2,3,0:T(4,128)} %maximum_bitcast_fusion), calls=%async_computation.2 | async-start | bytes 8454144 | tf_op jit(solution)/shard_map/all_to_all | solution.py:43
  207.3 0.6 bitcast_dynamic-update-slice_fusion
  207.9 47.2 %all-to-all-done.2 = f32[16,128,4,129]{1,2,3,0:T(4,128)} async-done(((f32[16,128,4,129]{1,2,3,0:T(4,128)}), f32[16,128,4,129]{1,2,3,0:T(4,128)}, u32[]{:S(2)}, u32[]{:S(2)}) %all-to-all-start.2) | async-done | bytes 4227104 | tf_op jit(solution)/shard_map/all_to_all | solution.py:43
  255.1 2.9 %reduce_sum.63 = f32[128,4,129]{0,1,2:T(4,128)S(1)} reduce(f32[16,128,4,129]{1,2,3,0:T(4,128)} %all-to-all-done.2, f32[]{:T(128)} %constant.71.clone.1), dimensions={0}, to_apply=%region_7.8 | reduce | flops 990720 | bytes 4491268 | tf_op jit(solution)/shard_map/reduce_sum | solution.py:44
  258.0 0.8 copy.143
  (113 shorter events, 3.4 us)
Async XLA Ops:
  1.8 71.2 %copy-start = (bf16[1,12,32,2,512]{4,3,2,1,0:T(2,128)(2,1)}, bf16[1,12,32,2,512]{4,3,2,1,0:T(2,128)(2,1)S(1)}, u32[]{:S(2)}) copy-start(bf16[1,12,32,2,512]{4,3,2,1,0:T(2,128)(2,1)S(1)} %copy.204) | copy-start | bytes 2359300
  2.9 8.9 %collective-permute-start = (bf16[128,512]{0,1:T(8,128)(2,1)S(1)}, bf16[128,512]{0,1:T(8,128)(2,1)S(1)}, u32[]{:S(2)}, u32[]{:S(2)}) collective-permute-start(bf16[128,512]{0,1:T(8,128)(2,1)S(1)} %bitcast.119), channel_id=1, source_target_pairs={{0,8},{8,16},{16,24},{24,32},{32,40},{40,48},{48,56},{56,64},{64,7... | collective-permute-start | bytes 393224 | tf_op jit(solution)/shard_map/ppermute | solution.py:124
  11.8 53.8 %copy-start.1 = (bf16[128,512]{0,1:T(8,128)(2,1)}, bf16[128,512]{0,1:T(8,128)(2,1)S(1)}, u32[]{:S(2)}) copy-start(bf16[128,512]{0,1:T(8,128)(2,1)S(1)} %collective-permute-done) | copy-start | bytes 393220
  11.8 8.3 %collective-permute-start.1 = (bf16[128,512]{0,1:T(8,128)(2,1)S(1)}, bf16[128,512]{0,1:T(8,128)(2,1)S(1)}, u32[]{:S(2)}, u32[]{:S(2)}) collective-permute-start(bf16[128,512]{0,1:T(8,128)(2,1)S(1)} %collective-permute-done), channel_id=1, source_target_pairs={{0,8},{8,16},{16,24},{24,32},{32,40},{40,48},{48,56},{56,64},{64,7... | collective-permute-start | bytes 393224 | tf_op jit(solution)/shard_map/ppermute | solution.py:124
  20.1 45.5 %copy-start.3 = (bf16[128,512]{0,1:T(8,128)(2,1)}, bf16[128,512]{0,1:T(8,128)(2,1)S(1)}, u32[]{:S(2)}) copy-start(bf16[128,512]{0,1:T(8,128)(2,1)S(1)} %collective-permute-done.1) | copy-start | bytes 393220
  20.1 8.3 %collective-permute-start.2 = (bf16[128,512]{0,1:T(8,128)(2,1)S(1)}, bf16[128,512]{0,1:T(8,128)(2,1)S(1)}, u32[]{:S(2)}, u32[]{:S(2)}) collective-permute-start(bf16[128,512]{0,1:T(8,128)(2,1)S(1)} %collective-permute-done.1), channel_id=1, source_target_pairs={{0,8},{8,16},{16,24},{24,32},{32,40},{40,48},{48,56},{56,64},{64,7... | collective-permute-start | bytes 393224 | tf_op jit(solution)/shard_map/ppermute | solution.py:124
  28.4 37.2 %copy-start.5 = (bf16[128,512]{0,1:T(8,128)(2,1)}, bf16[128,512]{0,1:T(8,128)(2,1)S(1)}, u32[]{:S(2)}) copy-start(bf16[128,512]{0,1:T(8,128)(2,1)S(1)} %collective-permute-done.2) | copy-start | bytes 393220
  28.4 8.3 %collective-permute-start.3 = (bf16[128,512]{0,1:T(8,128)(2,1)S(1)}, bf16[128,512]{0,1:T(8,128)(2,1)S(1)}, u32[]{:S(2)}, u32[]{:S(2)}) collective-permute-start(bf16[128,512]{0,1:T(8,128)(2,1)S(1)} %collective-permute-done.2), channel_id=1, source_target_pairs={{0,8},{8,16},{16,24},{24,32},{32,40},{40,48},{48,56},{56,64},{64,7... | collective-permute-start | bytes 393224 | tf_op jit(solution)/shard_map/ppermute | solution.py:124
  29.8 42.3 %copy-start.22 = (s32[1,4]{1,0:T(1,128)S(1)}, s32[1,4]{1,0:T(1,128)}, u32[]{:S(2)}) copy-start(s32[1,4]{1,0:T(1,128)} %param.11) | copy-start | bytes 52
  36.6 43.8 %copy-start.7 = (bf16[128,512]{0,1:T(8,128)(2,1)}, bf16[128,512]{0,1:T(8,128)(2,1)S(1)}, u32[]{:S(2)}) copy-start(bf16[128,512]{0,1:T(8,128)(2,1)S(1)} %collective-permute-done.3) | copy-start | bytes 393220
  36.6 8.3 %collective-permute-start.4 = (bf16[128,512]{0,1:T(8,128)(2,1)S(1)}, bf16[128,512]{0,1:T(8,128)(2,1)S(1)}, u32[]{:S(2)}, u32[]{:S(2)}) collective-permute-start(bf16[128,512]{0,1:T(8,128)(2,1)S(1)} %collective-permute-done.3), channel_id=1, source_target_pairs={{0,8},{8,16},{16,24},{24,32},{32,40},{40,48},{48,56},{56,64},{64,7... | collective-permute-start | bytes 393224 | tf_op jit(solution)/shard_map/ppermute | solution.py:124
  44.9 9.4 %copy-start.9 = (bf16[128,512]{0,1:T(8,128)(2,1)}, bf16[128,512]{0,1:T(8,128)(2,1)S(1)}, u32[]{:S(2)}) copy-start(bf16[128,512]{0,1:T(8,128)(2,1)S(1)} %collective-permute-done.4) | copy-start | bytes 393220
  44.9 8.7 %collective-permute-start.5 = (bf16[128,512]{0,1:T(8,128)(2,1)S(1)}, bf16[128,512]{0,1:T(8,128)(2,1)}, u32[]{:S(2)}, u32[]{:S(2)}) collective-permute-start(bf16[128,512]{0,1:T(8,128)(2,1)S(1)} %collective-permute-done.4), channel_id=1, source_target_pairs={{0,8},{8,16},{16,24},{24,32},{32,40},{40,48},{48,56},{56,64},{64,7... | collective-permute-start | bytes 393224 | tf_op jit(solution)/shard_map/ppermute | solution.py:124
  53.6 10.0 %collective-permute-start.6 = (bf16[128,512]{0,1:T(8,128)(2,1)}, bf16[128,512]{0,1:T(8,128)(2,1)}, u32[]{:S(2)}, u32[]{:S(2)}) collective-permute-start(bf16[128,512]{0,1:T(8,128)(2,1)} %collective-permute-done.5), channel_id=1, source_target_pairs={{0,8},{8,16},{16,24},{24,32},{32,40},{40,48},{48,56},{56,64},{64,7... | collective-permute-start | bytes 393224 | tf_op jit(solution)/shard_map/ppermute | solution.py:124
  63.6 8.5 %collective-permute-start.7 = (bf16[128,512]{0,1:T(8,128)(2,1)}, bf16[128,512]{0,1:T(8,128)(2,1)S(1)}, u32[]{:S(2)}, u32[]{:S(2)}) collective-permute-start(bf16[128,512]{0,1:T(8,128)(2,1)} %collective-permute-done.6), channel_id=1, source_target_pairs={{0,8},{8,16},{16,24},{24,32},{32,40},{40,48},{48,56},{56,64},{64,7... | collective-permute-start | bytes 393224 | tf_op jit(solution)/shard_map/ppermute | solution.py:124
  65.5 40.6 %all-to-all-start = ((bf16[8,2,32769]{2,1,0:T(2,128)(2,1)}), bf16[8,2,32769]{2,1,0:T(2,128)(2,1)S(1)}, u32[]{:S(2)}, u32[]{:S(2)}) async-start(bf16[8,2,32769]{2,1,0:T(2,128)(2,1)} %pad_maximum_fusion), calls=%async_computation | async-start | bytes 2105344 | tf_op jit(solution)/shard_map/all_to_all | solution.py:17
  72.1 34.0 %copy-start.11 = (bf16[128,512]{0,1:T(8,128)(2,1)}, bf16[128,512]{0,1:T(8,128)(2,1)S(1)}, u32[]{:S(2)}) copy-start(bf16[128,512]{0,1:T(8,128)(2,1)S(1)} %collective-permute-done.7) | copy-start | bytes 393220
  72.1 8.4 %collective-permute-start.8 = (bf16[128,512]{0,1:T(8,128)(2,1)S(1)}, bf16[128,512]{0,1:T(8,128)(2,1)S(1)}, u32[]{:S(2)}, u32[]{:S(2)}) collective-permute-start(bf16[128,512]{0,1:T(8,128)(2,1)S(1)} %collective-permute-done.7), channel_id=1, source_target_pairs={{0,8},{8,16},{16,24},{24,32},{32,40},{40,48},{48,56},{56,64},{64,7... | collective-permute-start | bytes 393224 | tf_op jit(solution)/shard_map/ppermute | solution.py:124
  80.5 25.7 %copy-start.13 = (bf16[128,512]{0,1:T(8,128)(2,1)}, bf16[128,512]{0,1:T(8,128)(2,1)S(1)}, u32[]{:S(2)}) copy-start(bf16[128,512]{0,1:T(8,128)(2,1)S(1)} %collective-permute-done.8) | copy-start | bytes 393220
  80.5 8.3 %collective-permute-start.9 = (bf16[128,512]{0,1:T(8,128)(2,1)S(1)}, bf16[128,512]{0,1:T(8,128)(2,1)S(1)}, u32[]{:S(2)}, u32[]{:S(2)}) collective-permute-start(bf16[128,512]{0,1:T(8,128)(2,1)S(1)} %collective-permute-done.8), channel_id=1, source_target_pairs={{0,8},{8,16},{16,24},{24,32},{32,40},{40,48},{48,56},{56,64},{64,7... | collective-permute-start | bytes 393224 | tf_op jit(solution)/shard_map/ppermute | solution.py:124
  88.7 17.4 %copy-start.15 = (bf16[128,512]{0,1:T(8,128)(2,1)}, bf16[128,512]{0,1:T(8,128)(2,1)S(1)}, u32[]{:S(2)}) copy-start(bf16[128,512]{0,1:T(8,128)(2,1)S(1)} %collective-permute-done.9) | copy-start | bytes 393220
  88.7 8.3 %collective-permute-start.10 = (bf16[128,512]{0,1:T(8,128)(2,1)S(1)}, bf16[128,512]{0,1:T(8,128)(2,1)S(1)}, u32[]{:S(2)}, u32[]{:S(2)}) collective-permute-start(bf16[128,512]{0,1:T(8,128)(2,1)S(1)} %collective-permute-done.9), channel_id=1, source_target_pairs={{0,8},{8,16},{16,24},{24,32},{32,40},{40,48},{48,56},{56,64},{64,7... | collective-permute-start | bytes 393224 | tf_op jit(solution)/shard_map/ppermute | solution.py:124
  97.0 9.1 %copy-start.17 = (bf16[128,512]{0,1:T(8,128)(2,1)}, bf16[128,512]{0,1:T(8,128)(2,1)S(1)}, u32[]{:S(2)}) copy-start(bf16[128,512]{0,1:T(8,128)(2,1)S(1)} %collective-permute-done.10) | copy-start | bytes 393220
  97.0 8.4 %collective-permute-start.11 = (bf16[128,512]{0,1:T(8,128)(2,1)S(1)}, bf16[128,512]{0,1:T(8,128)(2,1)}, u32[]{:S(2)}, u32[]{:S(2)}) collective-permute-start(bf16[128,512]{0,1:T(8,128)(2,1)S(1)} %collective-permute-done.10), channel_id=1, source_target_pairs={{0,8},{8,16},{16,24},{24,32},{32,40},{40,48},{48,56},{56,64},{64,7... | collective-permute-start | bytes 393224 | tf_op jit(solution)/shard_map/ppermute | solution.py:124
  105.4 8.6 %collective-permute-start.12 = (bf16[128,512]{0,1:T(8,128)(2,1)}, bf16[128,512]{0,1:T(8,128)(2,1)}, u32[]{:S(2)}, u32[]{:S(2)}) collective-permute-start(bf16[128,512]{0,1:T(8,128)(2,1)} %collective-permute-done.11), channel_id=1, source_target_pairs={{0,8},{8,16},{16,24},{24,32},{32,40},{40,48},{48,56},{56,64},{64,7... | collective-permute-start | bytes 393224 | tf_op jit(solution)/shard_map/ppermute | solution.py:124
  114.0 9.4 %collective-permute-start.13 = (bf16[128,512]{0,1:T(8,128)(2,1)}, bf16[128,512]{0,1:T(8,128)(2,1)}, u32[]{:S(2)}, u32[]{:S(2)}) collective-permute-start(bf16[128,512]{0,1:T(8,128)(2,1)} %collective-permute-done.12), channel_id=1, source_target_pairs={{0,8},{8,16},{16,24},{24,32},{32,40},{40,48},{48,56},{56,64},{64,7... | collective-permute-start | bytes 393224 | tf_op jit(solution)/shard_map/ppermute | solution.py:124
  114.4 27.8 %copy-start.6 = (bf16[128,512]{0,1:T(8,128)(2,1)S(1)}, bf16[128,512]{0,1:T(8,128)(2,1)}, u32[]{:S(2)}) copy-start(bf16[128,512]{0,1:T(8,128)(2,1)} %copy-done.5) | copy-start | bytes 393220
  114.4 27.8 %copy-start.4 = (bf16[128,512]{0,1:T(8,128)(2,1)S(1)}, bf16[128,512]{0,1:T(8,128)(2,1)}, u32[]{:S(2)}) copy-start(bf16[128,512]{0,1:T(8,128)(2,1)} %copy-done.3) | copy-start | bytes 393220
  114.4 27.8 %copy-start.2 = (bf16[128,512]{0,1:T(8,128)(2,1)S(1)}, bf16[128,512]{0,1:T(8,128)(2,1)}, u32[]{:S(2)}) copy-start(bf16[128,512]{0,1:T(8,128)(2,1)} %copy-done.1) | copy-start | bytes 393220
  114.4 32.7 %copy-start.10 = (bf16[128,512]{0,1:T(8,128)(2,1)S(1)}, bf16[128,512]{0,1:T(8,128)(2,1)}, u32[]{:S(2)}) copy-start(bf16[128,512]{0,1:T(8,128)(2,1)} %copy-done.9) | copy-start | bytes 393220
  114.4 32.7 %copy-start.8 = (bf16[128,512]{0,1:T(8,128)(2,1)S(1)}, bf16[128,512]{0,1:T(8,128)(2,1)}, u32[]{:S(2)}) copy-start(bf16[128,512]{0,1:T(8,128)(2,1)} %copy-done.7) | copy-start | bytes 393220
  114.5 30.7 %copy-start.18 = (bf16[128,512]{0,1:T(8,128)(2,1)S(1)}, bf16[128,512]{0,1:T(8,128)(2,1)}, u32[]{:S(2)}) copy-start(bf16[128,512]{0,1:T(8,128)(2,1)} %copy-done.17) | copy-start | bytes 393220
  114.5 30.7 %copy-start.16 = (bf16[128,512]{0,1:T(8,128)(2,1)S(1)}, bf16[128,512]{0,1:T(8,128)(2,1)}, u32[]{:S(2)}) copy-start(bf16[128,512]{0,1:T(8,128)(2,1)} %copy-done.15) | copy-start | bytes 393220
  114.5 30.7 %copy-start.14 = (bf16[128,512]{0,1:T(8,128)(2,1)S(1)}, bf16[128,512]{0,1:T(8,128)(2,1)}, u32[]{:S(2)}) copy-start(bf16[128,512]{0,1:T(8,128)(2,1)} %copy-done.13) | copy-start | bytes 393220
  114.5 30.7 %copy-start.12 = (bf16[128,512]{0,1:T(8,128)(2,1)S(1)}, bf16[128,512]{0,1:T(8,128)(2,1)}, u32[]{:S(2)}) copy-start(bf16[128,512]{0,1:T(8,128)(2,1)} %copy-done.11) | copy-start | bytes 393220
  123.5 8.5 %collective-permute-start.14 = (bf16[128,512]{0,1:T(8,128)(2,1)}, bf16[128,512]{0,1:T(8,128)(2,1)S(1)}, u32[]{:S(2)}, u32[]{:S(2)}) collective-permute-start(bf16[128,512]{0,1:T(8,128)(2,1)} %collective-permute-done.13), channel_id=1, source_target_pairs={{0,8},{8,16},{16,24},{24,32},{32,40},{40,48},{48,56},{56,64},{64,7... | collective-permute-start | bytes 393224 | tf_op jit(solution)/shard_map/ppermute | solution.py:124
  147.5 7.3 %copy-start.19 = (pred[128,136]{0,1:T(8,128)(4,1)S(1)}, pred[128,136]{0,1:T(8,128)(4,1)}, u32[]{:S(2)}) copy-start(pred[128,136]{0,1:T(8,128)(4,1)} %pad_add_fusion) | copy-start | bytes 52228
  147.5 7.3 %copy-start.20 = (bf16[8,2,4,128]{3,0,2,1:T(8,128)(2,1)S(1)}, bf16[8,2,4,128]{3,0,2,1:T(8,128)(2,1)}, u32[]{:S(2)}) copy-start(bf16[8,2,4,128]{3,0,2,1:T(8,128)(2,1)} %copy.131) | copy-start | bytes 49156
  158.5 12.6 %slice-start = ((s8[4456448]{0:T(1024)(128)(4,1)}), s8[262144]{0:T(1024)(128)(4,1)S(1)}, s32[]{:S(2)}) async-start(s8[4456448]{0:T(1024)(128)(4,1)} %bitcast.112), calls=%async_computation.3 | async-start | bytes 524288
  158.5 19.2 %all-to-all-start.1 = ((f32[16,128,4,16]{1,3,2,0:T(8,128)}), f32[16,128,4,16]{1,3,2,0:T(8,128)S(1)}, u32[]{:S(2)}, u32[]{:S(2)}) async-start(f32[16,128,4,16]{1,3,2,0:T(8,128)} %broadcast_in_dim.138), calls=%async_computation.1 | async-start | bytes 1048576 | tf_op jit(solution)/shard_map/all_to_all | solution.py:26
  162.5 8.6 %slice-start.1 = ((s8[4456448]{0:T(1024)(128)(4,1)}), s8[4194304]{0:T(1024)(128)(4,1)S(1)}, s32[]{:S(2)}) async-start(s8[4456448]{0:T(1024)(128)(4,1)} %bitcast.112), calls=%async_computation.4 | async-start | bytes 8388608
  199.5 7.8 %copy-start.21 = (bf16[1,8,2,512]{3,2,1,0:T(2,128)(2,1)S(1)}, bf16[1,8,2,512]{3,2,1,0:T(2,128)(2,1)}, u32[]{:S(2)}) copy-start(bf16[1,8,2,512]{3,2,1,0:T(2,128)(2,1)} %param.9) | copy-start | bytes 49156
  199.5 55.6 %all-to-all-start.2 = ((f32[16,128,4,129]{1,2,3,0:T(4,128)}), f32[16,128,4,129]{1,2,3,0:T(4,128)}, u32[]{:S(2)}, u32[]{:S(2)}) async-start(f32[16,128,4,129]{1,2,3,0:T(4,128)} %maximum_bitcast_fusion), calls=%async_computation.2 | async-start | bytes 8454144 | tf_op jit(solution)/shard_map/all_to_all | solution.py:43
